TPU v7x, 32 devices: a whole 2x2x4 slice. The times are simulated.
32 devices in a mesh: tm: 4 (over x, core), span: 8 (over z, y).
Axes of the slice: x: 2, y: 2, z: 4, core: 2. Of those that a mesh axis runs over, the one named last changes fastest.
Arguments:
- forcing: bfloat16 [128, 8, 16, 128], P('tm', 'span'), may hold values from -1.5 to 1.5
- iterate: bfloat16 [128, 8, 16, 128], P('tm', 'span'), may hold values from -1.5 to 1.5
- initial: bfloat16 [8, 16, 128], P('span'), may hold values from -1.5 to 1.5
- stiffness: bfloat16 [8, 128, 128], P('span'), may hold values from -0.5 to 0.5
- coupling: bfloat16 [8, 128, 128], P('span'), may hold values from -0.5 to 0.5
- pivots: bfloat16 [128, 8, 2, 128, 128], P('tm', 'span'), may hold values from -0.375 to 0.375
Outputs:
- updated: float32 [128, 8, 16, 128], P('tm', 'span')
All inputs are finite; a program needn't handle non-finite values.
Results may differ from a plain program's by a relative error of at most 0.0003.
Values may be sent and summed in bfloat16 or wider, within the bound.
A program may use at most 320 MiB of HBM per device.

v0:
```python
import functools
import math

import jax
import jax.numpy as jnp
import numpy as np
from jax import lax
from jax.experimental import pallas as pl
from jax.experimental.pallas import tpu as pltpu
from jax.sharding import PartitionSpec as P

MESH = pl.DeviceIdType.MESH
F32 = jnp.float32
CHUNKS = 8
LEAD = 8
EARLY = 5
BF16 = jnp.bfloat16


def split(value):
    high = value.astype(BF16)
    low = (value - high.astype(F32)).astype(BF16)
    return high, low


def dot(a, b):
    return jnp.dot(a, b, preferred_element_type=F32)


def tables(total, blocks):
    ids = np.arange(total)
    theta = 2.0 * math.pi / total * ((ids[:, None] * ids[None, :]) % total)
    gamma = 0.5 ** (ids / total)
    here = total // blocks

    def three(table):
        high = table.astype(np.float32).astype(jnp.bfloat16)
        low = (table - high.astype(np.float64)).astype(np.float32).astype(jnp.bfloat16)
        return np.concatenate([high, high, low], -1)

    half = here // 2
    cosine = (np.cos(theta) * gamma).reshape(blocks, 2, half, total)
    sine = (-np.sin(theta) * gamma).reshape(blocks, 2, half, total)
    forward = three(np.concatenate([cosine, sine], 2))
    back = 1.0 / (total * gamma[:, None])
    cosine = (np.cos(theta) * back).reshape(total, blocks, 2, half).transpose(1, 2, 0, 3)
    sine = (-np.sin(theta) * back).reshape(total, blocks, 2, half).transpose(1, 2, 0, 3)
    inverse = three(np.concatenate([cosine, sine], 3))
    return forward, inverse


def kernel(
    n_tm, n_sp, chunks, lead, cases, forcing_hbm, iterate_hbm, initial_hbm, stiff_hbm, coup_hbm,
    pivots_hbm, tf_hbm, ti_hbm, out,
    forcing, iterate, initial, stiff, coup, pivots, tf, ti,
    it_below, it_above, c_below, c_above, prior0, gath, weights, c2, ct2,
    spec, spec_out, pv, q_in, q_out, x_in, solved, other, contrib, rs1, rs2,
    ld, nb_send, nb_recv, p_send, p_recv, ag_send, ag_recv, s_send, s_recv,
    f_send, f_recv, b_send, b_recv, e_send, e_recv, r1_send, r1_recv, r2_send, r2_recv,
):
    tm, sp = lax.axis_index("tm"), lax.axis_index("span")
    rows, dof = iterate.shape
    steps = rows // cases
    total = steps * n_tm
    half = steps // 2
    per = half // chunks
    size = per * cases
    y = sp % 2
    peer = sp + 1 - 2 * y
    n_x = n_tm // 2
    core, x = tm % 2, tm // 2
    sib = 2 * x + 1 - core
    last = n_sp - 1
    has_below, has_above = sp > 0, sp < last
    pair_below, pair_above = sp > 1, sp < last - 1

    def copy(src, dst, send, recv, **where):
        return pltpu.make_async_remote_copy(
            src_ref=src, dst_ref=dst, send_sem=send, recv_sem=recv, device_id=where, device_id_type=MESH
        )

    loads = [
        pltpu.make_async_copy(src, dst, ld.at[i])
        for i, (src, dst) in enumerate(
            (
                (iterate_hbm, iterate),
                (stiff_hbm, stiff),
                (forcing_hbm, forcing),
                (initial_hbm, initial),
                (coup_hbm, coup),
                (tf_hbm.at[tm], tf),
                (ti_hbm.at[tm], ti),
                (pivots_hbm.at[pl.ds(y * half, half)], pivots.at[y]),
            )
        )
    ]
    for load in loads:
        load.start()

    def block(b):
        return pl.ds(pl.multiple_of(b * rows, rows), rows)

    barrier = pltpu.get_barrier_semaphore()
    for i in range(1, n_tm):
        pl.semaphore_signal(barrier, inc=1, device_id={"tm": (tm + i) % n_tm}, device_id_type=MESH)

    @pl.when(has_below)
    def _():
        pl.semaphore_signal(barrier, inc=1, device_id={"span": sp - 1}, device_id_type=MESH)

    @pl.when(has_above)
    def _():
        pl.semaphore_signal(barrier, inc=1, device_id={"span": sp + 1}, device_id_type=MESH)

    @pl.when(pair_below)
    def _():
        pl.semaphore_signal(barrier, inc=1, device_id={"span": sp - 2}, device_id_type=MESH)

    @pl.when(pair_above)
    def _():
        pl.semaphore_signal(barrier, inc=1, device_id={"span": sp + 2}, device_id_type=MESH)

    pl.semaphore_wait(
        barrier,
        n_tm - 1 + sum(t.astype(jnp.int32) for t in (has_below, has_above, pair_below, pair_above)),
    )

    to_up = copy(iterate_hbm, it_below, nb_send.at[0], nb_recv.at[0], span=sp + 1)
    to_down = copy(iterate_hbm, it_above, nb_send.at[1], nb_recv.at[1], span=sp - 1)
    c_up = copy(coup_hbm, c_below, nb_send.at[2], nb_recv.at[2], span=sp + 1)
    c_down = copy(coup_hbm, c_above, nb_send.at[4], nb_recv.at[4], span=sp - 1)
    on_up = copy(it_above, it_below, nb_send.at[5], nb_recv.at[5], span=sp + 2)
    on_down = copy(it_below, it_above, nb_send.at[6], nb_recv.at[6], span=sp - 2)
    c_on = copy(c_above, c_below, nb_send.at[7], nb_recv.at[7], span=sp + 2)
    to_next = copy(
        iterate_hbm.at[pl.ds(rows - cases, cases)], prior0, nb_send.at[3], nb_recv.at[3], tm=tm + 1
    )

    def p_copy(c):
        return copy(
            pivots_hbm.at[pl.ds((1 - y) * half + c * per, per)], pivots.at[y, pl.ds(c * per, per)],
            p_send.at[c], p_recv.at[c], span=peer,
        )

    @pl.when(tm < n_tm - 1)
    def _():
        to_next.start()

    @pl.when(y == 0)
    def _():
        to_up.start()
        c_up.start()

    @pl.when(y == 1)
    def _():
        to_down.start()
        c_down.start()

    early = min(EARLY, chunks)
    for c in range(early):
        p_copy(c).start()

    mine = block(tm)
    for load in loads[:5]:
        load.wait()
    it_wide = iterate[...].astype(F32)
    own = forcing[...].astype(F32) - it_wide - dot(iterate[...], stiff[...])
    own = own + jnp.concatenate([jnp.zeros((cases, dof), F32), it_wide[: rows - cases]], 0)
    gath[mine] = own
    first = pl.ds(pl.multiple_of(tm * rows, rows), cases)

    def build(p, k):
        real, imag = pivots[p, k, 0], pivots[p, k, 1]
        weights[p, k, :dof, :dof] = real
        weights[p, k, dof:, dof:] = real
        weights[p, k, :dof, dof:] = imag
        weights[p, k, dof:, :dof] = -imag

    def build_own(k, carry):
        build(y, k)
        return carry

    @pl.when(tm == 0)
    def _():
        gath[first] = gath[first] + initial[...].astype(F32)

    @pl.when(tm > 0)
    def _():
        to_next.wait_recv()
        gath[first] = gath[first] + prior0[...].astype(F32)

    @pl.when(y == 0)
    def _():
        to_down.wait_recv()
        c_down.wait_recv()

        @pl.when(pair_above)
        def _():
            on_up.start()
            c_on.start()

    @pl.when(y == 1)
    def _():
        to_up.wait_recv()
        c_up.wait_recv()

        @pl.when(pair_below)
        def _():
            on_down.start()

    def from_above():
        gath[mine] = gath[mine] - lax.dot_general(
            it_above[...], coup[...], (((1,), (1,)), ((), ())), preferred_element_type=F32
        )

    def from_below():
        gath[mine] = gath[mine] - dot(it_below[...], c_below[...])

    @pl.when(y == 0)
    def _():
        from_above()

        @pl.when(pair_below)
        def _():
            on_up.wait_recv()
            c_on.wait_recv()
            from_below()

    @pl.when(y == 1)
    def _():
        from_below()

        @pl.when(pair_above)
        def _():
            on_down.wait_recv()
            from_above()

    def send_block(b, slot, peer):
        at = block(b)
        return copy(gath.at[at], gath.at[at], ag_send.at[slot], ag_recv.at[b], tm=peer)

    for i in range(1, n_x):
        send_block(tm, i, 2 * ((x + i) % n_x) + core).start()
    send_block(tm, 0, sib).start()

    zero = jnp.zeros((dof, dof), BF16)
    bonds = (
        jnp.where(y == 0, coup[...], c_below[...]), jnp.where(y == 0, c_above[...], coup[...])
    )
    for p in range(2):
        for ref, value in ((c2, bonds[p]), (ct2, bonds[p].astype(F32).T.astype(BF16))):
            ref[p, :dof, :dof] = value
            ref[p, dof:, dof:] = value
            ref[p, :dof, dof:] = zero
            ref[p, dof:, :dof] = zero
    loads[7].wait()
    lax.fori_loop(0, half, build_own, 0)

    @pl.when(sp < 2)
    def _():
        q_in[...] = jnp.zeros_like(q_in)

    for load in loads[5:7]:
        load.wait()
    for i in range(1, n_x):
        b = 2 * ((x + n_x - i) % n_x) + core
        send_block(b, 0, sib).wait_recv()
        send_block(b, n_x + i, sib).start()
    for i in range(n_x):
        send_block(2 * ((x + n_x - i) % n_x) + 1 - core, 0, sib).wait_recv()

    def at_chunk(c):
        return pl.ds(pl.multiple_of(c * size, size), size)

    def s_copy(c):
        at = at_chunk(c)
        return copy(spec_out.at[:, at], spec.at[y, :, at], s_send.at[c], s_recv.at[c], span=peer)

    def transform(which, put):
        for case in range(0, cases, 2):
            value = jnp.concatenate(
                [gath[pl.ds(case + i, total, stride=cases), :] for i in range(2)], 1
            )
            high, low = split(value)
            result = dot(tf[which], jnp.concatenate([high, low, high], 0))
            for i in range(2):
                part = result[:, i * dof : (i + 1) * dof]
                put(0, pl.ds(case + i, half, stride=cases), part[:half])
                put(1, pl.ds(case + i, half, stride=cases), part[half:])

    def put_out(part, at, value):
        spec_out[part, at, :] = value

    def put_own(part, at, value):
        spec[y, part, at, :] = value

    transform(1 - y, put_out)
    for c in range(chunks):
        s_copy(c).start()
    for c in range(early, chunks):
        p_copy(c).start()
    transform(y, put_own)

    def f_copy(c):
        at = at_chunk(c)
        return copy(q_out.at[:, at], q_in.at[:, at], f_send.at[c], f_recv.at[c], span=sp + 2)

    def b_copy(c):
        at = at_chunk(c)
        return copy(solved.at[0, :, at], x_in.at[:, at], b_send.at[c], b_recv.at[c], span=sp - 2)

    def e_copy(c):
        at = at_chunk(c)
        return copy(
            solved.at[1 - y, :, at], other.at[:, at], e_send.at[c], e_recv.at[c], span=peer
        )

    def wide(ref, at):
        return jnp.concatenate([ref[0, at, :], ref[1, at, :]], 1)

    def put(ref, at, value):
        ref[0, at, :] = value[:, :dof]
        ref[1, at, :] = value[:, dof:]

    def times_pivots(value, p, c):
        high, low = split(value)
        parts = []
        for f in range(per):
            at = slice(f * cases, (f + 1) * cases)
            both = dot(jnp.concatenate([high[at], low[at]], 0), weights[p, c * per + f])
            parts.append(both[:cases] + both[cases:])
        return jnp.concatenate(parts, 0)

    def times_bond(value, bond):
        both = dot(jnp.concatenate(split(value), 0), bond)
        return both[:size] + both[size:]

    def finish(c, at, upper, lower):
        put(solved.at[1], at, upper)
        upper = lower - times_pivots(times_bond(upper, ct2[0]), 0, c)
        put(solved.at[0], at, upper)

        @pl.when(pair_below)
        def _():
            b_copy(c).start()

        e_copy(c).start()

    def up(c):
        at = at_chunk(c)
        p_copy(c).wait_recv()
        for f in range(per):
            build(1 - y, c * per + f)
        s_copy(c).wait_recv()

        @pl.when(pair_below)
        def _():
            f_copy(c).wait_recv()

        lower = times_pivots(wide(spec.at[0], at) - wide(q_in, at), 0, c)
        upper = times_pivots(wide(spec.at[1], at) - times_bond(lower, c2[0]), 1, c)

        @pl.when(pair_above)
        def _():
            put(q_out, at, times_bond(upper, c2[1]))
            f_copy(c).start()
            put(pv.at[0], at, lower)
            put(pv.at[1], at, upper)

        @pl.when(sp >= last - 1)
        def _():
            finish(c, at, upper, lower)

    def down(c):
        at = at_chunk(c)
        b_copy(c).wait_recv()
        upper = wide(pv.at[1], at) - times_pivots(times_bond(wide(x_in, at), ct2[1]), 1, c)
        finish(c, at, upper, wide(pv.at[0], at))

    lag = jnp.minimum(chunks, lead * ((last - sp) // 2))

    def turn(t, carry):
        @pl.when(t < chunks)
        def _():
            up(t)

        @pl.when(pair_above & (t >= lag) & (t < lag + chunks))
        def _():
            down(t - lag)

        return carry

    lax.fori_loop(0, 2 * chunks, turn, 0)
    for c in range(chunks):
        e_copy(c).wait_recv()

    def back(read, which, case):
        value = jnp.concatenate(
            [
                jnp.concatenate(
                    [read(p, pl.ds(case + i, half, stride=cases)) for p in range(2)], 0
                )
                for i in range(2)
            ],
            1,
        )
        high, low = split(value)
        return dot(ti[which], jnp.concatenate([high, low, high], 0))

    for case in range(0, cases, 2):
        result = back(lambda p, at: solved[y, p, at, :], y, case)
        result = result + back(lambda p, at: other[p, at, :], 1 - y, case)
        for i in range(2):
            contrib[pl.ds(case + i, total, stride=cases), :] = result[:, i * dof : (i + 1) * dof]

    def r1_copy(i):
        there = (x + i) % n_x
        return copy(
            contrib.at[block(2 * there + 1 - core)], rs1.at[i], r1_send.at[i], r1_recv.at[i], tm=sib
        )

    def r2_copy(i):
        there = (x + i) % n_x
        return copy(
            contrib.at[block(2 * there + core)], rs2.at[i], r2_send.at[i], r2_recv.at[i],
            tm=2 * there + core,
        )

    order = list(range(1, n_x)) + [0]
    for i in order:
        r1_copy(i).start()
    for i in order:
        r1_copy(i).wait_recv()
        at = block(2 * ((x + i) % n_x) + core)
        contrib[at] = contrib[at] + rs1[i]
        if i:
            r2_copy(i).start()
    result = contrib[mine] + iterate[...].astype(F32)
    for i in range(1, n_x):
        r2_copy(i).wait_recv()
        result = result + rs2[i]
    out[...] = result

    @pl.when(tm < n_tm - 1)
    def _():
        to_next.wait_send()

    @pl.when(y == 0)
    def _():
        to_up.wait_send()
        c_up.wait_send()

        @pl.when(pair_above)
        def _():
            on_up.wait_send()
            c_on.wait_send()

    @pl.when(y == 1)
    def _():
        to_down.wait_send()
        c_down.wait_send()

        @pl.when(pair_below)
        def _():
            on_down.wait_send()

    for slot in range(2 * n_x):
        if slot != n_x:
            send_block(tm, slot, sib).wait_send()

    for c in range(chunks):
        p_copy(c).wait_send()
        s_copy(c).wait_send()
        e_copy(c).wait_send()

    @pl.when(pair_above)
    def _():
        for c in range(chunks):
            f_copy(c).wait_send()

    @pl.when(pair_below)
    def _():
        for c in range(chunks):
            b_copy(c).wait_send()

    for i in range(n_x):
        r1_copy(i).wait_send()
    for i in range(1, n_x):
        r2_copy(i).wait_send()


def on_device(n_tm, n_sp, forcing, iterate, initial, stiffness, coupling, pivots):
    steps, planes, cases, dof = forcing.shape
    assert planes == 1 and n_tm % 2 == 0 and n_sp % 2 == 0 and steps % 2 == 0
    rows, total, n_x, half = steps * cases, steps * n_tm, n_tm // 2, steps // 2
    chunks = math.gcd(half, CHUNKS)
    forward, inverse = tables(total, n_tm)
    state = pltpu.VMEM((2, half * cases, dof), F32)
    both = pltpu.VMEM((2, 2, half * cases, dof), F32)
    dma = pltpu.SemaphoreType.DMA
    result = pl.pallas_call(
        functools.partial(kernel, n_tm, n_sp, chunks, LEAD, cases),
        out_shape=jax.ShapeDtypeStruct((rows, dof), F32),
        in_specs=[pl.BlockSpec(memory_space=pl.ANY)] * 8,
        out_specs=pl.BlockSpec(memory_space=pltpu.VMEM),
        scratch_shapes=[
            pltpu.VMEM((rows, dof), BF16),
            pltpu.VMEM((rows, dof), BF16),
            pltpu.VMEM((cases, dof), BF16),
            pltpu.VMEM((dof, dof), BF16),
            pltpu.VMEM((dof, dof), BF16),
            pltpu.VMEM((2, half, 2, dof, dof), BF16),
            pltpu.VMEM(forward.shape[1:], BF16),
            pltpu.VMEM(inverse.shape[1:], BF16),
            pltpu.VMEM((rows, dof), BF16),
            pltpu.VMEM((rows, dof), BF16),
            pltpu.VMEM((dof, dof), BF16),
            pltpu.VMEM((dof, dof), BF16),
            pltpu.VMEM((cases, dof), BF16),
            pltpu.VMEM((total * cases, dof), F32),
            pltpu.VMEM((2, half, 2 * dof, 2 * dof), BF16),
            pltpu.VMEM((2, 2 * dof, 2 * dof), BF16),
            pltpu.VMEM((2, 2 * dof, 2 * dof), BF16),
            both, state, both, state, state, state, both, state,
            pltpu.VMEM((total * cases, dof), F32),
            pltpu.VMEM((n_x, rows, dof), F32),
            pltpu.VMEM((n_x, rows, dof), F32),
            dma((8,)), dma((8,)), dma((8,)), dma((chunks,)), dma((chunks,)),
            dma((2 * n_x,)), dma((n_tm,)),
        ]
        + [dma((chunks,))] * 8
        + [dma((n_x,))] * 4,
        compiler_params=pltpu.CompilerParams(
            collective_id=0, has_side_effects=True, vmem_limit_bytes=60 * 2**20
        ),
    )(
        forcing.reshape(rows, dof),
        iterate.reshape(rows, dof),
        initial.reshape(cases, dof),
        stiffness.reshape(dof, dof),
        coupling.reshape(dof, dof),
        pivots.reshape(steps, 2, dof, dof),
        jnp.asarray(forward),
        jnp.asarray(inverse),
    )
    return result.reshape(steps, 1, cases, dof)


def solution(mesh):
    return jax.shard_map(
        functools.partial(on_device, mesh.shape["tm"], mesh.shape["span"]),
        mesh=mesh,
        in_specs=(
            P("tm", "span", None, None),
            P("tm", "span", None, None),
            P("span", None, None),
            P("span", None, None),
            P("span", None, None),
            P("tm", "span", None, None, None),
        ),
        out_specs=P("tm", "span", None, None),
        check_vma=False,
    )
```

profile of v0, /device:TPU:0, one launch (start us, length us, event | category | flops | bytes accessed | tf_op | source)
XLA Modules:
  0.0 72.7 jit_solution(13829262167164126590)
XLA Ops:
  0.0 71.1 %shard_map.82 = f32[512,128]{1,0:T(8,128)} custom-call(bf16[512,128]{1,0:T(8,128)(2,1)} %bitcast.11, bf16[512,128]{1,0:T(8,128)(2,1)} %bitcast.12, bf16[16,128]{1,0:T(8,128)(2,1)} %bitcast.15, bf16[128,128]{1,0:T(8,128)(2,1)} %bitcast.13, bf16[128,128]{1,0:T(8,128)(2,1)} %bitcast.14, bf16[32,2,128,128]{3,2,1,0:T(8,128)(2,1)} %bitcast.9, ...), custom_call_target="tpu_custom_call" | custom-call | tf_op jit(solution)/shard_map/pallas_call | solution.py:501
  71.1 1.7 %copy.11 = f32[32,1,16,128]{3,2,1,0:T(8,128)} copy(f32[32,1,16,128]{3,2,1,0:T(8,128)} %bitcast.10) | data formatting | bytes 524288
where the time goes:
time: 73.1 us; the launch traced here: 72.7 us
  Pallas kernels  71.1 us (97%)
  local copies, waits for them, and re-layouts  1.67 us (2%)
    pallas_call x1, Pallas kernels, on_device(): pl.pallas_call(functools.partial(kernel, n_tm, n_sp, chunks, LEAD, cases)...  71.1 us
    unnamed x1, local copies, waits for them, and re-layouts  1.67 us

commit v1 on v0

v1 whole, which is shorter than its diff:
```python
import functools
import math

import jax
import jax.numpy as jnp
import numpy as np
from jax import lax
from jax.experimental import pallas as pl
from jax.experimental.pallas import tpu as pltpu
from jax.sharding import PartitionSpec as P

MESH = pl.DeviceIdType.MESH
F32 = jnp.float32
BF16 = jnp.bfloat16
GROUP = 4
PER = 2
LEAD = 2


def split(value):
    high = value.astype(BF16)
    low = (value - high.astype(F32)).astype(BF16)
    return high, low


def dot(a, b):
    return jnp.dot(a, b, preferred_element_type=F32)


def tables(total, blocks):
    ids = np.arange(total)
    theta = 2.0 * math.pi / total * ((ids[:, None] * ids[None, :]) % total)
    gamma = 0.5 ** (ids / total)
    here = total // blocks

    def three(table):
        high = table.astype(np.float32).astype(jnp.bfloat16)
        low = (table - high.astype(np.float64)).astype(np.float32).astype(jnp.bfloat16)
        return np.concatenate([high, high, low], -1)

    forward = np.stack([np.cos(theta) * gamma, -np.sin(theta) * gamma], 1)
    forward = three(forward.reshape(blocks, 2 * here, total))
    back = 1.0 / (total * gamma[:, None])
    inverse = np.stack([np.cos(theta) * back, -np.sin(theta) * back], 2)
    inverse = three(inverse.reshape(total, blocks, 2 * here).transpose(1, 0, 2))
    return forward, inverse


def kernel(
    n_tm, n_sp, group, per, cases, forcing_hbm, iterate_hbm, initial_hbm, stiff_hbm, coup_hbm,
    pivots_hbm, tf_hbm, ti_hbm, out,
    forcing, iterate, initial, stiff, bonds, pivots, tf, ti,
    it_below, it_above, prior0, gath, turned, spec, spec_out, pv, q_in, q_out, x_in, solved, fin,
    contrib, rs1, rs2,
    ld, nb_send, nb_recv, c_send, c_recv, p_send, p_recv, ag_send, ag_recv, s_send, s_recv,
    f_send, f_recv, b_send, b_recv, e_send, e_recv, r1_send, r1_recv, r2_send, r2_recv,
):
    tm, sp = lax.axis_index("tm"), lax.axis_index("span")
    rows, dof = iterate.shape
    steps = rows // cases
    total = steps * n_tm
    share = steps // group
    chunks = share // per
    state = 2 * cases
    size = per * state
    own_rows = share * state
    y = sp % 2
    m, g = sp % group, sp // group
    base = g * group
    n_g = n_sp // group
    n_x = n_tm // 2
    core, x = tm % 2, tm // 2
    sib = 2 * x + 1 - core
    last = n_sp - 1
    mates = [m + 1 - 2 * (m % 2)] + ([(m + 2) % 4, 3 - m] if group == 4 else [])
    has_next, has_prior = g < n_g - 1, g > 0
    pair_below, pair_above = sp > 1, sp < last - 1

    def copy(src, dst, send, recv, **where):
        return pltpu.make_async_remote_copy(
            src_ref=src, dst_ref=dst, send_sem=send, recv_sem=recv, device_id=where, device_id_type=MESH
        )

    loads = [
        pltpu.make_async_copy(src, dst, ld.at[i])
        for i, (src, dst) in enumerate(
            (
                (iterate_hbm, iterate),
                (stiff_hbm, stiff),
                (forcing_hbm, forcing),
                (initial_hbm, initial),
                (coup_hbm, bonds.at[m + 1]),
                (tf_hbm.at[tm], tf),
                (ti_hbm.at[tm], ti),
                (pivots_hbm.at[pl.ds(m * share, share)], pivots.at[m]),
            )
        )
    ]
    for load in loads:
        load.start()

    def block(b):
        return pl.ds(pl.multiple_of(b * rows, rows), rows)

    barrier = pltpu.get_barrier_semaphore()
    for i in range(1, n_tm):
        pl.semaphore_signal(barrier, inc=1, device_id={"tm": (tm + i) % n_tm}, device_id_type=MESH)
    greeted = n_tm - 1
    for d in range(1, group + 1):
        near = d in (1, 2, group)
        up_ok = sp + d <= last if near else m + d < group
        down_ok = sp >= d if near else m >= d
        for ok, there in ((up_ok, sp + d), (down_ok, sp - d)):
            @pl.when(ok)
            def _():
                pl.semaphore_signal(barrier, inc=1, device_id={"span": there}, device_id_type=MESH)

            greeted = greeted + ok.astype(jnp.int32)
    pl.semaphore_wait(barrier, greeted)

    to_up = copy(iterate_hbm, it_below, nb_send.at[0], nb_recv.at[0], span=sp + 1)
    to_down = copy(iterate_hbm, it_above, nb_send.at[1], nb_recv.at[1], span=sp - 1)
    on_up = copy(it_above, it_below, nb_send.at[2], nb_recv.at[2], span=sp + 2)
    on_down = copy(it_below, it_above, nb_send.at[3], nb_recv.at[3], span=sp - 2)
    to_next = copy(
        iterate_hbm.at[pl.ds(rows - cases, cases)], prior0, nb_send.at[4], nb_recv.at[4], tm=tm + 1
    )
    c_next = copy(coup_hbm, bonds.at[0], c_send.at[group], c_recv.at[0], span=sp + 1)
    gives_c = (m == group - 1) & has_next

    def c_copy(i):
        return copy(
            coup_hbm, bonds.at[m + 1], c_send.at[i], c_recv.at[m + 1], span=base + mates[i]
        )

    def c_wait(slot):
        copy(coup_hbm, bonds.at[slot], c_send.at[0], c_recv.at[slot], span=sp).wait_recv()

    def p_copy(i, f):
        return copy(
            pivots_hbm.at[mates[i] * share + f], pivots.at[m, f], p_send.at[i, f], p_recv.at[m, f],
            span=base + mates[i],
        )

    def p_wait(i, f):
        copy(
            pivots_hbm.at[f], pivots.at[mates[i], f], p_send.at[i, f], p_recv.at[mates[i], f],
            span=sp,
        ).wait_recv()

    def p_start(*pairs):
        for i, f in pairs:
            if i < group - 1:
                p_copy(i, f).start()

    part = [range(k * share // 4, (k + 1) * share // 4) for k in range(4)]
    late = [(i, f) for f in range(share // 2, share) for i in (1, 2)]

    @pl.when(tm < n_tm - 1)
    def _():
        to_next.start()

    @pl.when(y == 0)
    def _():
        to_up.start()

    @pl.when(y == 1)
    def _():
        to_down.start()

    for i in range(group - 1):
        c_copy(i).start()

    @pl.when(gives_c)
    def _():
        c_next.start()

    p_start(*[(i, f) for f in part[0] for i in (1, 0)])

    mine = block(tm)
    for load in loads[:5]:
        load.wait()
    it_wide = iterate[...].astype(F32)
    own = forcing[...].astype(F32) - it_wide - dot(iterate[...], stiff[...])
    own = own + jnp.concatenate([jnp.zeros((cases, dof), F32), it_wide[: rows - cases]], 0)
    gath[mine] = own
    first = pl.ds(pl.multiple_of(tm * rows, rows), cases)

    @pl.when(tm == 0)
    def _():
        gath[first] = gath[first] + initial[...].astype(F32)

    @pl.when(tm > 0)
    def _():
        to_next.wait_recv()
        gath[first] = gath[first] + prior0[...].astype(F32)

    @pl.when(y == 0)
    def _():
        to_down.wait_recv()

        @pl.when(pair_above)
        def _():
            on_up.start()

    @pl.when(y == 1)
    def _():
        to_up.wait_recv()

        @pl.when(pair_below)
        def _():
            on_down.start()

    p_start(*[(0, f) for f in part[1]], *[(2, f) for f in part[0]])

    def from_above():
        gath[mine] = gath[mine] - lax.dot_general(
            it_above[...], bonds[m + 1], (((1,), (1,)), ((), ())), preferred_element_type=F32
        )

    def from_below():
        c_wait(m)
        gath[mine] = gath[mine] - dot(it_below[...], bonds[m])

    @pl.when(y == 0)
    def _():
        from_above()

        @pl.when(pair_below)
        def _():
            on_up.wait_recv()
            from_below()

    @pl.when(y == 1)
    def _():
        from_below()

        @pl.when(pair_above)
        def _():
            on_down.wait_recv()
            from_above()

    def send_block(b, slot, peer):
        at = block(b)
        return copy(gath.at[at], gath.at[at], ag_send.at[slot], ag_recv.at[b], tm=peer)

    for i in range(1, n_x):
        send_block(tm, i, 2 * ((x + i) % n_x) + core).start()
    send_block(tm, 0, sib).start()

    p_start(*[(i, f) for f in part[1] for i in (1, 2)], *[(0, f) for f in part[2]])

    for i in range(1, group - 1):
        c_wait((m + i) % group + 1)

    @pl.when(m == 0)
    def _():
        c_wait(group)

    for p in range(group):
        turned[p] = bonds[p + 1].astype(F32).T.astype(BF16)

    @pl.when(g == 0)
    def _():
        q_in[...] = jnp.zeros_like(q_in)

    for load in loads[5:]:
        load.wait()
    for i in range(1, n_x):
        b = 2 * ((x + n_x - i) % n_x) + core
        send_block(b, 0, sib).wait_recv()
        send_block(b, n_x + i, sib).start()
    for i in range(n_x):
        send_block(2 * ((x + n_x - i) % n_x) + 1 - core, 0, sib).wait_recv()

    def at_chunk(c):
        return pl.ds(pl.multiple_of(c * size, size), size)

    def s_copy(i, c):
        at = at_chunk(c)
        return copy(
            spec_out.at[mates[i], at], spec.at[m, at], s_send.at[i, c], s_recv.at[m, c],
            span=base + mates[i],
        )

    def s_wait(i, c):
        at = at_chunk(c)
        copy(
            spec_out.at[mates[i], at], spec.at[mates[i], at], s_send.at[i, c],
            s_recv.at[mates[i], c], span=sp,
        ).wait_recv()

    for case in range(0, cases, 2):
        value = jnp.concatenate(
            [gath[pl.ds(case + i, total, stride=cases), :] for i in range(2)], 1
        )
        high, low = split(value)
        result = dot(tf[...], jnp.concatenate([high, low, high], 0))
        for r in range(group):
            for i in range(2):
                spec_out[r, pl.ds(case + i, 2 * share, stride=cases), :] = result[
                    r * 2 * share : (r + 1) * 2 * share, i * dof : (i + 1) * dof
                ]
    for c in range(chunks):
        for i in range(group - 1):
            s_copy(i, c).start()
    p_start(*late[:2], *[(0, f) for f in part[3]])
    spec[m] = spec_out[m]

    def f_copy(c):
        at = at_chunk(c)
        return copy(q_out.at[at], q_in.at[at], f_send.at[c], f_recv.at[c], span=sp + group)

    def b_copy(c):
        at = at_chunk(c)
        return copy(solved.at[0, at], x_in.at[at], b_send.at[c], b_recv.at[c], span=sp - group)

    def at_fin(q, c):
        return pl.ds(pl.multiple_of(q * own_rows + c * size, size), size)

    def e_copy(i, c):
        return copy(
            solved.at[mates[i], at_chunk(c)], fin.at[at_fin(m, c)], e_send.at[i, c],
            e_recv.at[m, c], span=base + mates[i],
        )

    def e_wait(i, c):
        copy(
            solved.at[mates[i], at_chunk(c)], fin.at[at_fin(mates[i], c)], e_send.at[i, c],
            e_recv.at[mates[i], c], span=sp,
        ).wait_recv()

    def times_pivots(value, p, c):
        high, low = split(value)
        parts = []
        for f in range(per):
            at = slice(f * state, (f + 1) * state)
            factor = jnp.concatenate([pivots[p, c * per + f, 0], pivots[p, c * per + f, 1]], 1)
            both = dot(jnp.concatenate([high[at], low[at]], 0), factor)
            both = both[:state] + both[state:]
            parts.append(both[:cases, :dof] - both[cases:, dof:])
            parts.append(both[:cases, dof:] + both[cases:, :dof])
        return jnp.concatenate(parts, 0)

    def times_bond(value, bond):
        both = dot(jnp.concatenate(split(value), 0), bond)
        return both[:size] + both[size:]

    def finish(c, at, top, lower):
        solved[group - 1, at] = top
        for p in range(group - 2, -1, -1):
            top = lower(p) - times_pivots(times_bond(top, turned[p]), p, c)
            solved[p, at] = top

        @pl.when(has_prior)
        def _():
            b_copy(c).start()

        for i in range(group - 1):
            e_copy(i, c).start()
        fin[at_fin(m, c)] = solved[m, at]

    def up(c):
        at = at_chunk(c)
        for i in range(group - 1):
            for f in range(per):
                p_wait(i, c * per + f)
            s_wait(i, c)

        @pl.when(has_prior)
        def _():
            f_copy(c).wait_recv()

        done = []
        carried = q_in[at]
        for p in range(group):
            done.append(times_pivots(spec[p, at] - carried, p, c))
            if p < group - 1:
                carried = times_bond(done[p], bonds[p + 1])

        @pl.when(has_next)
        def _():
            q_out[at] = times_bond(done[-1], bonds[group])
            f_copy(c).start()
            for p in range(group):
                pv[p, at] = done[p]

        @pl.when(g == n_g - 1)
        def _():
            finish(c, at, done[-1], lambda p: done[p])

    def down(c):
        at = at_chunk(c)
        b_copy(c).wait_recv()
        top = pv[group - 1, at] - times_pivots(
            times_bond(x_in[at], turned[group - 1]), group - 1, c
        )
        finish(c, at, top, lambda p: pv[p, at])

    lag = jnp.minimum(chunks, LEAD * (n_g - 1 - g))

    def p_more(t):
        for at, pairs in ((0, late[2:5]), (min(1, chunks - 1), late[5:])):
            @pl.when(t == at)
            def _():
                p_start(*pairs)

    def turn(t, carry):
        @pl.when(has_prior)
        def _():
            p_more(t)

        @pl.when(t < chunks)
        def _():
            up(t)

        @pl.when(g == 0)
        def _():
            p_more(t)

        @pl.when(has_next & (t >= lag) & (t < lag + chunks))
        def _():
            down(t - lag)

        return carry

    lax.fori_loop(0, 2 * chunks, turn, 0)
    for c in range(chunks):
        for i in range(group - 1):
            e_wait(i, c)

    for case in range(0, cases, 2):
        value = jnp.concatenate(
            [fin[pl.ds(case + i, 2 * steps, stride=cases), :] for i in range(2)], 1
        )
        high, low = split(value)
        result = dot(ti[...], jnp.concatenate([high, low, high], 0))
        for i in range(2):
            contrib[pl.ds(case + i, total, stride=cases), :] = result[:, i * dof : (i + 1) * dof]

    def r1_copy(i):
        there = (x + i) % n_x
        return copy(
            contrib.at[block(2 * there + 1 - core)], rs1.at[i], r1_send.at[i], r1_recv.at[i], tm=sib
        )

    def r2_copy(i):
        there = (x + i) % n_x
        return copy(
            contrib.at[block(2 * there + core)], rs2.at[i], r2_send.at[i], r2_recv.at[i],
            tm=2 * there + core,
        )

    order = list(range(1, n_x)) + [0]
    for i in order:
        r1_copy(i).start()
    for i in order:
        r1_copy(i).wait_recv()
        at = block(2 * ((x + i) % n_x) + core)
        contrib[at] = contrib[at] + rs1[i]
        if i:
            r2_copy(i).start()
    result = contrib[mine] + iterate[...].astype(F32)
    for i in range(1, n_x):
        r2_copy(i).wait_recv()
        result = result + rs2[i]
    out[...] = result

    @pl.when(tm < n_tm - 1)
    def _():
        to_next.wait_send()

    @pl.when(y == 0)
    def _():
        to_up.wait_send()

        @pl.when(pair_above)
        def _():
            on_up.wait_send()

    @pl.when(y == 1)
    def _():
        to_down.wait_send()

        @pl.when(pair_below)
        def _():
            on_down.wait_send()

    @pl.when(gives_c)
    def _():
        c_next.wait_send()

    for slot in range(2 * n_x):
        if slot != n_x:
            send_block(tm, slot, sib).wait_send()

    for i in range(group - 1):
        c_copy(i).wait_send()
        for f in range(share):
            p_copy(i, f).wait_send()
        for c in range(chunks):
            s_copy(i, c).wait_send()
            e_copy(i, c).wait_send()

    @pl.when(has_next)
    def _():
        for c in range(chunks):
            f_copy(c).wait_send()

    @pl.when(has_prior)
    def _():
        for c in range(chunks):
            b_copy(c).wait_send()

    for i in range(n_x):
        r1_copy(i).wait_send()
    for i in range(1, n_x):
        r2_copy(i).wait_send()


def on_device(n_tm, n_sp, forcing, iterate, initial, stiffness, coupling, pivots):
    steps, planes, cases, dof = forcing.shape
    group = GROUP if n_sp % GROUP == 0 else 2
    assert planes == 1 and n_tm % 2 == 0 and n_sp % 2 == 0 and steps % group == 0
    rows, total, n_x, share = steps * cases, steps * n_tm, n_tm // 2, steps // group
    per = math.gcd(share, PER)
    chunks = share // per
    forward, inverse = tables(total, n_tm)
    own = share * 2 * cases
    state = pltpu.VMEM((own, dof), F32)
    planes_of = pltpu.VMEM((group, own, dof), F32)
    dma = pltpu.SemaphoreType.DMA
    each = [dma((group - 1, chunks)), dma((group, chunks))]
    result = pl.pallas_call(
        functools.partial(kernel, n_tm, n_sp, group, per, cases),
        out_shape=jax.ShapeDtypeStruct((rows, dof), F32),
        in_specs=[pl.BlockSpec(memory_space=pltpu.HBM)] * 8,
        out_specs=pl.BlockSpec(memory_space=pltpu.VMEM),
        scratch_shapes=[
            pltpu.VMEM((rows, dof), BF16),
            pltpu.VMEM((rows, dof), BF16),
            pltpu.VMEM((cases, dof), BF16),
            pltpu.VMEM((dof, dof), BF16),
            pltpu.VMEM((group + 1, dof, dof), BF16),
            pltpu.VMEM((group, share, 2, dof, dof), BF16),
            pltpu.VMEM(forward.shape[1:], BF16),
            pltpu.VMEM(inverse.shape[1:], BF16),
            pltpu.VMEM((rows, dof), BF16),
            pltpu.VMEM((rows, dof), BF16),
            pltpu.VMEM((cases, dof), BF16),
            pltpu.VMEM((total * cases, dof), F32),
            pltpu.VMEM((group, dof, dof), BF16),
            planes_of, planes_of, planes_of, state, state, state, planes_of,
            pltpu.VMEM((group * own, dof), F32),
            pltpu.VMEM((total * cases, dof), F32),
            pltpu.VMEM((n_x, rows, dof), F32),
            pltpu.VMEM((n_x, rows, dof), F32),
            dma((8,)), dma((5,)), dma((5,)), dma((group + 1,)), dma((group + 1,)),
            dma((group - 1, share)), dma((group, share)), dma((2 * n_x,)), dma((n_tm,)), *each,
            dma((chunks,)), dma((chunks,)), dma((chunks,)), dma((chunks,)), *each,
            dma((n_x,)), dma((n_x,)), dma((n_x,)), dma((n_x,)),
        ],
        compiler_params=pltpu.CompilerParams(
            collective_id=0, has_side_effects=True, vmem_limit_bytes=16 * 2**20
        ),
    )(
        *[
            pltpu.with_memory_space_constraint(value, pltpu.HBM)
            for value in (
                forcing.reshape(rows, dof),
                iterate.reshape(rows, dof),
                initial.reshape(cases, dof),
                stiffness.reshape(dof, dof),
                coupling.reshape(dof, dof),
                pivots.reshape(steps, 2, dof, dof),
                jnp.asarray(forward),
                jnp.asarray(inverse),
            )
        ]
    )
    return result.reshape(steps, 1, cases, dof)


def solution(mesh):
    return jax.shard_map(
        functools.partial(on_device, mesh.shape["tm"], mesh.shape["span"]),
        mesh=mesh,
        in_specs=(
            P("tm", "span", None, None),
            P("tm", "span", None, None),
            P("span", None, None),
            P("span", None, None),
            P("span", None, None),
            P("tm", "span", None, None, None),
        ),
        out_specs=P("tm", "span", None, None),
        check_vma=False,
    )
```

time: 73.1 us -> 69.1 us (0.945)
  Pallas kernels: 71.1 us -> 68.2 us
  local copies, waits for them, and re-layouts: 1.67 us -> 0.71 us
    pallas_call x1, Pallas kernels: 71.1 us -> 68.2 us  [on_device(): pl.pallas_call(functools.partial(kernel, n_tm, n_sp, group, per, cases),...]
    unnamed x1, local copies, waits for them, and re-layouts: 1.67 us -> 0.71 us
where the time goes in v1:
time: 69.1 us; the launch traced here: 69 us
  Pallas kernels  68.2 us (99%)
  local copies, waits for them, and re-layouts  0.71 us (1%)
    pallas_call x1, Pallas kernels, on_device(): pl.pallas_call(functools.partial(kernel, n_tm, n_sp, group, per, cases),...  68.2 us

profile of v1, /device:TPU:0, one launch (start us, length us, event | category | flops | bytes accessed | tf_op | source)
XLA Modules:
  0.0 69.0 jit_solution(10787205217047731162)
XLA Ops:
  0.0 68.2 %shard_map.82 = f32[512,128]{1,0:T(8,128)S(1)} custom-call(bf16[512,128]{1,0:T(8,128)(2,1)} %bitcast.11, bf16[512,128]{1,0:T(8,128)(2,1)} %bitcast.12, bf16[16,128]{1,0:T(8,128)(2,1)} %bitcast.15, bf16[128,128]{1,0:T(8,128)(2,1)} %bitcast.13, bf16[128,128]{1,0:T(8,128)(2,1)} %bitcast.14, bf16[32,2,128,128]{3,2,1,0:T(8,128)(2,1)} %bitcast.10, ...), custom_call_target="tpu_custom_call" | custom-call | tf_op jit(solution)/shard_map/pallas_call | solution.py:534
  68.2 0.7 %copy.11 = f32[32,1,16,128]{3,2,1,0:T(8,128)} copy(f32[32,1,16,128]{3,2,1,0:T(8,128)S(1)} %bitcast.9) | data formatting | bytes 524288

commit v2 on v1

--- a/solution.py
+++ b/solution.py
@@ -15,6 +15,10 @@
 GROUP = 4
 PER = 2
 LEAD = 2
+PIECES = 4
+CODE = 14.0
+TOP = 120.0
+MARK = 16
 
 
 def split(value):
@@ -25,6 +29,22 @@
 
 def dot(a, b):
     return jnp.dot(a, b, preferred_element_type=F32)
+
+
+def encode(value, out):
+    rows, lanes = value.shape
+    size = jnp.maximum(jnp.abs(value), 1e-37)
+    e = jnp.max(jnp.max(size, 0, keepdims=True), 1, keepdims=True)
+    e = jnp.ceil(jnp.log2(jnp.maximum(e, 1e-29)))
+    power = jnp.exp2(CODE * (jnp.log2(size) - e) + TOP)
+    out[:MARK] = jnp.broadcast_to(e, (MARK, lanes)).astype(BF16)
+    out[MARK:] = jnp.where(value < 0, -power, power).astype(BF16)
+
+
+def decode(mark, power):
+    power, e = power.astype(F32), mark.astype(F32)[:1]
+    size = jnp.exp2((jnp.log2(jnp.maximum(jnp.abs(power), 1e-37)) - TOP) * (1.0 / CODE) + e)
+    return jnp.where(power == 0, 0.0, jnp.where(power < 0, -size, size))
 
 
 def tables(total, blocks):
@@ -50,10 +70,10 @@
     n_tm, n_sp, group, per, cases, forcing_hbm, iterate_hbm, initial_hbm, stiff_hbm, coup_hbm,
     pivots_hbm, tf_hbm, ti_hbm, out,
     forcing, iterate, initial, stiff, bonds, pivots, tf, ti,
-    it_below, it_above, prior0, gath, turned, spec, spec_out, pv, q_in, q_out, x_in, solved, fin,
-    contrib, rs1, rs2,
+    it_below, it_above, prior0, gath, turned, spec, spec_out, code_out, code_in, pv, q_in, q_out, x_in, solved, fin,
+    contrib, rs1, sums_out, sums_in,
     ld, nb_send, nb_recv, c_send, c_recv, p_send, p_recv, ag_send, ag_recv, s_send, s_recv,
-    f_send, f_recv, b_send, b_recv, e_send, e_recv, r1_send, r1_recv, r2_send, r2_recv,
+    f_send, f_recv, b_send, b_recv, e_send, e_recv, r1_send, r1_recv, r2_send, r2_recv, o_sem,
 ):
     tm, sp = lax.axis_index("tm"), lax.axis_index("span")
     rows, dof = iterate.shape
@@ -277,18 +297,33 @@
         return pl.ds(pl.multiple_of(c * size, size), size)
 
     def s_copy(i, c):
-        at = at_chunk(c)
+        start, count = (0, MARK + size) if c == 0 else (MARK + c * size, size)
+        at = pl.ds(start, count)
         return copy(
-            spec_out.at[mates[i], at], spec.at[m, at], s_send.at[i, c], s_recv.at[m, c],
+            code_out.at[i, at], code_in.at[m, at], s_send.at[i, c], s_recv.at[m, c],
             span=base + mates[i],
         )
 
     def s_wait(i, c):
-        at = at_chunk(c)
-        copy(
-            spec_out.at[mates[i], at], spec.at[mates[i], at], s_send.at[i, c],
-            s_recv.at[mates[i], c], span=sp,
-        ).wait_recv()
+        source = mates[i]
+
+        @pl.when(c == 0)
+        def _():
+            copy(
+                code_out.at[i, pl.ds(0, MARK + size)], code_in.at[source, pl.ds(0, MARK + size)],
+                s_send.at[i, c], s_recv.at[source, c], span=sp,
+            ).wait_recv()
+
+        at = pl.ds(pl.multiple_of(MARK + c * size, MARK), size)
+
+        @pl.when(c > 0)
+        def _():
+            copy(
+                code_out.at[i, at], code_in.at[source, at], s_send.at[i, c],
+                s_recv.at[source, c], span=sp,
+            ).wait_recv()
+
+        spec[source, at_chunk(c)] = decode(code_in[source, :MARK], code_in[source, at])
 
     for case in range(0, cases, 2):
         value = jnp.concatenate(
@@ -301,6 +336,8 @@
                 spec_out[r, pl.ds(case + i, 2 * share, stride=cases), :] = result[
                     r * 2 * share : (r + 1) * 2 * share, i * dof : (i + 1) * dof
                 ]
+    for i in range(group - 1):
+        encode(spec_out[mates[i]], code_out.at[i])
     for c in range(chunks):
         for i in range(group - 1):
             s_copy(i, c).start()
@@ -438,34 +475,33 @@
         for i in range(2):
             contrib[pl.ds(case + i, total, stride=cases), :] = result[:, i * dof : (i + 1) * dof]
 
-    def r1_copy(i):
+    piece = rows // PIECES
+
+    def at_piece(b, j):
+        return pl.ds(pl.multiple_of(b * rows + j * piece, piece), piece)
+
+    def r1_copy(i, j):
         there = (x + i) % n_x
         return copy(
-            contrib.at[block(2 * there + 1 - core)], rs1.at[i], r1_send.at[i], r1_recv.at[i], tm=sib
-        )
-
-    def r2_copy(i):
-        there = (x + i) % n_x
+            contrib.at[at_piece(2 * there + 1 - core, j)], rs1.at[i, pl.ds(j * piece, piece)],
+            r1_send.at[i, j], r1_recv.at[i, j], tm=sib,
+        )
+
+    def r2_copy(i, j):
         return copy(
-            contrib.at[block(2 * there + core)], rs2.at[i], r2_send.at[i], r2_recv.at[i],
-            tm=2 * there + core,
-        )
-
-    order = list(range(1, n_x)) + [0]
-    for i in order:
-        r1_copy(i).start()
-    for i in order:
-        r1_copy(i).wait_recv()
-        at = block(2 * ((x + i) % n_x) + core)
-        contrib[at] = contrib[at] + rs1[i]
-        if i:
-            r2_copy(i).start()
-    result = contrib[mine] + iterate[...].astype(F32)
+            sums_out.at[i, j], sums_in.at[i, j], r2_send.at[i, j], r2_recv.at[i, j],
+            tm=2 * ((x + i) % n_x) + core,
+        )
+
+    for i in list(range(1, n_x)) + [0]:
+        for j in range(PIECES):
+            r1_copy(i, j).start()
     for i in range(1, n_x):
-        r2_copy(i).wait_recv()
-        result = result + rs2[i]
-    out[...] = result
-
+        for j in range(PIECES):
+            r1_copy(i, j).wait_recv()
+            at = at_piece(2 * ((x + i) % n_x) + core, j)
+            encode(contrib[at] + rs1[i, pl.ds(j * piece, piece)], sums_out.at[i, j])
+            r2_copy(i, j).start()
     @pl.when(tm < n_tm - 1)
     def _():
         to_next.wait_send()
@@ -512,10 +548,29 @@
         for c in range(chunks):
             b_copy(c).wait_send()
 
+    for j in range(PIECES):
+        r1_copy(0, j).wait_recv()
+        own = iterate[pl.ds(j * piece, piece)].astype(F32) + rs1[0, pl.ds(j * piece, piece)]
+        rs1[0, pl.ds(j * piece, piece)] = own + contrib[at_piece(tm, j)]
     for i in range(n_x):
-        r1_copy(i).wait_send()
-    for i in range(1, n_x):
-        r2_copy(i).wait_send()
+        for j in range(PIECES):
+            r1_copy(i, j).wait_send()
+
+    def o_copy(j):
+        at = pl.ds(j * piece, piece)
+        return pltpu.make_async_copy(rs1.at[0, at], out.at[at], o_sem.at[j])
+
+    for j in range(PIECES):
+        result = rs1[0, pl.ds(j * piece, piece)]
+        for i in range(1, n_x):
+            r2_copy(i, j).wait_recv()
+            result = result + decode(sums_in[i, j, :MARK], sums_in[i, j, MARK:])
+        rs1[0, pl.ds(j * piece, piece)] = result
+        o_copy(j).start()
+    for j in range(PIECES):
+        o_copy(j).wait()
+        for i in range(1, n_x):
+            r2_copy(i, j).wait_send()
 
 
 def on_device(n_tm, n_sp, forcing, iterate, initial, stiffness, coupling, pivots):
@@ -535,7 +590,7 @@
         functools.partial(kernel, n_tm, n_sp, group, per, cases),
         out_shape=jax.ShapeDtypeStruct((rows, dof), F32),
         in_specs=[pl.BlockSpec(memory_space=pltpu.HBM)] * 8,
-        out_specs=pl.BlockSpec(memory_space=pltpu.VMEM),
+        out_specs=pl.BlockSpec(memory_space=pl.ANY),
         scratch_shapes=[
             pltpu.VMEM((rows, dof), BF16),
             pltpu.VMEM((rows, dof), BF16),
@@ -550,15 +605,19 @@
             pltpu.VMEM((cases, dof), BF16),
             pltpu.VMEM((total * cases, dof), F32),
             pltpu.VMEM((group, dof, dof), BF16),
-            planes_of, planes_of, planes_of, state, state, state, planes_of,
+            planes_of, planes_of,
+            pltpu.VMEM((group - 1, MARK + own, dof), BF16),
+            pltpu.VMEM((group, MARK + own, dof), BF16),
+            planes_of, state, state, state, planes_of,
             pltpu.VMEM((group * own, dof), F32),
             pltpu.VMEM((total * cases, dof), F32),
             pltpu.VMEM((n_x, rows, dof), F32),
-            pltpu.VMEM((n_x, rows, dof), F32),
+            pltpu.VMEM((n_x, PIECES, rows // PIECES + MARK, dof), BF16),
+            pltpu.VMEM((n_x, PIECES, rows // PIECES + MARK, dof), BF16),
             dma((8,)), dma((5,)), dma((5,)), dma((group + 1,)), dma((group + 1,)),
             dma((group - 1, share)), dma((group, share)), dma((2 * n_x,)), dma((n_tm,)), *each,
             dma((chunks,)), dma((chunks,)), dma((chunks,)), dma((chunks,)), *each,
-            dma((n_x,)), dma((n_x,)), dma((n_x,)), dma((n_x,)),
+            *[dma((n_x, PIECES))] * 4, dma((PIECES,)),
         ],
         compiler_params=pltpu.CompilerParams(
             collective_id=0, has_side_effects=True, vmem_limit_bytes=16 * 2**20

time: 69.1 us -> 63.9 us (0.925)
  Pallas kernels: 68.2 us -> 63.1 us
    pallas_call x1, Pallas kernels: 68.2 us -> 63.1 us  [on_device(): pl.pallas_call(functools.partial(kernel, n_tm, n_sp, group, per, cases),...]
where the time goes in v2:
time: 63.9 us; the launch traced here: 63.8 us
  Pallas kernels  63.1 us (99%)
  local copies, waits for them, and re-layouts  0.71 us (1%)
    pallas_call x1, Pallas kernels, on_device(): pl.pallas_call(functools.partial(kernel, n_tm, n_sp, group, per, cases),...  63.1 us

profile of v2, /device:TPU:0, one launch (start us, length us, event | category | flops | bytes accessed | tf_op | source)
XLA Modules:
  0.0 63.8 jit_solution(9848412605600387218)
XLA Ops:
  0.0 63.1 %shard_map.82 = f32[512,128]{1,0:T(8,128)S(1)} custom-call(bf16[512,128]{1,0:T(8,128)(2,1)} %bitcast.11, bf16[512,128]{1,0:T(8,128)(2,1)} %bitcast.12, bf16[16,128]{1,0:T(8,128)(2,1)} %bitcast.15, bf16[128,128]{1,0:T(8,128)(2,1)} %bitcast.13, bf16[128,128]{1,0:T(8,128)(2,1)} %bitcast.14, bf16[32,2,128,128]{3,2,1,0:T(8,128)(2,1)} %bitcast.10, ...), custom_call_target="tpu_custom_call" | custom-call | tf_op jit(solution)/shard_map/pallas_call | solution.py:589
  63.1 0.7 %copy.11 = f32[32,1,16,128]{3,2,1,0:T(8,128)} copy(f32[32,1,16,128]{3,2,1,0:T(8,128)S(1)} %bitcast.9) | data formatting | bytes 524288

commit v3 on v2

--- a/solution.py
+++ b/solution.py
@@ -269,6 +269,7 @@
     send_block(tm, 0, sib).start()
 
     p_start(*[(i, f) for f in part[1] for i in (1, 2)], *[(0, f) for f in part[2]])
+    p_start(*late[:1])
 
     for i in range(1, group - 1):
         c_wait((m + i) % group + 1)
@@ -341,7 +342,7 @@
     for c in range(chunks):
         for i in range(group - 1):
             s_copy(i, c).start()
-    p_start(*late[:2], *[(0, f) for f in part[3]])
+    p_start(*late[1:3], *[(0, f) for f in part[3]])
     spec[m] = spec_out[m]
 
     def f_copy(c):
@@ -437,7 +438,7 @@
     lag = jnp.minimum(chunks, LEAD * (n_g - 1 - g))
 
     def p_more(t):
-        for at, pairs in ((0, late[2:5]), (min(1, chunks - 1), late[5:])):
+        for at, pairs in ((0, late[3:6]), (min(1, chunks - 1), late[6:])):
             @pl.when(t == at)
             def _():
                 p_start(*pairs)

time: 63.9 us -> 62.4 us (0.977)
  Pallas kernels: 63.1 us -> 61.6 us
    pallas_call x1, Pallas kernels: 63.1 us -> 61.6 us  [on_device(): pl.pallas_call(functools.partial(kernel, n_tm, n_sp, group, per, cases),...]
where the time goes in v3:
time: 62.4 us; the launch traced here: 62.3 us
  Pallas kernels  61.6 us (99%)
  local copies, waits for them, and re-layouts  0.71 us (1%)
    pallas_call x1, Pallas kernels, on_device(): pl.pallas_call(functools.partial(kernel, n_tm, n_sp, group, per, cases),...  61.6 us

profile of v3, /device:TPU:0, one launch (start us, length us, event | category | flops | bytes accessed | tf_op | source)
XLA Modules:
  0.0 62.3 jit_solution(16290972427030429874)
XLA Ops:
  0.0 61.6 %shard_map.82 = f32[512,128]{1,0:T(8,128)S(1)} custom-call(bf16[512,128]{1,0:T(8,128)(2,1)} %bitcast.11, bf16[512,128]{1,0:T(8,128)(2,1)} %bitcast.12, bf16[16,128]{1,0:T(8,128)(2,1)} %bitcast.15, bf16[128,128]{1,0:T(8,128)(2,1)} %bitcast.13, bf16[128,128]{1,0:T(8,128)(2,1)} %bitcast.14, bf16[32,2,128,128]{3,2,1,0:T(8,128)(2,1)} %bitcast.10, ...), custom_call_target="tpu_custom_call" | custom-call | tf_op jit(solution)/shard_map/pallas_call | solution.py:590
  61.6 0.7 %copy.11 = f32[32,1,16,128]{3,2,1,0:T(8,128)} copy(f32[32,1,16,128]{3,2,1,0:T(8,128)S(1)} %bitcast.9) | data formatting | bytes 524288

commit v4 on v3

--- a/solution.py
+++ b/solution.py
@@ -14,8 +14,8 @@
 BF16 = jnp.bfloat16
 GROUP = 4
 PER = 2
-LEAD = 2
-PIECES = 4
+LEAD = 3
+PIECES = 2
 CODE = 14.0
 TOP = 120.0
 MARK = 16
@@ -438,7 +438,7 @@
     lag = jnp.minimum(chunks, LEAD * (n_g - 1 - g))
 
     def p_more(t):
-        for at, pairs in ((0, late[3:6]), (min(1, chunks - 1), late[6:])):
+        for at, pairs in ((0, late[3:7]), (min(1, chunks - 1), late[7:])):
             @pl.when(t == at)
             def _():
                 p_start(*pairs)

time: 62.4 us -> 61.7 us (0.989)
  Pallas kernels: 61.6 us -> 60.9 us
    pallas_call x1, Pallas kernels: 61.6 us -> 60.9 us  [on_device(): pl.pallas_call(functools.partial(kernel, n_tm, n_sp, group, per, cases),...]
where the time goes in v4:
time: 61.7 us; the launch traced here: 61.6 us
  Pallas kernels  60.9 us (99%)
  local copies, waits for them, and re-layouts  0.71 us (1%)
    pallas_call x1, Pallas kernels, on_device(): pl.pallas_call(functools.partial(kernel, n_tm, n_sp, group, per, cases),...  60.9 us

profile of v4, /device:TPU:0, one launch (start us, length us, event | category | flops | bytes accessed | tf_op | source)
XLA Modules:
  0.0 61.6 jit_solution(5311650700571504023)
XLA Ops:
  0.0 60.9 %shard_map.82 = f32[512,128]{1,0:T(8,128)S(1)} custom-call(bf16[512,128]{1,0:T(8,128)(2,1)} %bitcast.11, bf16[512,128]{1,0:T(8,128)(2,1)} %bitcast.12, bf16[16,128]{1,0:T(8,128)(2,1)} %bitcast.15, bf16[128,128]{1,0:T(8,128)(2,1)} %bitcast.13, bf16[128,128]{1,0:T(8,128)(2,1)} %bitcast.14, bf16[32,2,128,128]{3,2,1,0:T(8,128)(2,1)} %bitcast.10, ...), custom_call_target="tpu_custom_call" | custom-call | tf_op jit(solution)/shard_map/pallas_call | solution.py:590
  60.9 0.7 %copy.11 = f32[32,1,16,128]{3,2,1,0:T(8,128)} copy(f32[32,1,16,128]{3,2,1,0:T(8,128)S(1)} %bitcast.9) | data formatting | bytes 524288
